TPU v7x, 32 devices: a whole 2x2x4 slice. The times are simulated.
32 devices in a mesh: blk: 16 (over z, x, core), narrow: 2 (over y).
Axes of the slice: x: 2, y: 2, z: 4, core: 2. Of those that a mesh axis runs over, the one named last changes fastest.
Arguments:
- rhs: float32 [6144, 256], P('blk', 'narrow'), may hold values from -6 to 6
- zo: float32 [6144, 64], P('blk'), may hold values from -0.109375 to 0.109375
- e_diag: float32 [64, 96, 96], P('blk'), may hold values from -0.18 to 0.18
- a_off: float32 [64, 3, 96, 96], P('blk'), may hold values from -0.18 to 0.18
- e_off: float32 [64, 3, 96, 96], P('blk'), may hold values from -0.09 to 0.09
- col_index: int32 [64, 3], P('blk'), may hold values from 0 to 63, as said below
- inv_diag: float32 [2, 64, 96, 96], P(None, 'blk'), may hold values from -0.625 to 0.625
- shifts: float32 [2], replicated, may hold values from 0.5 to 2
Outputs:
- residual: float32 [6144, 256], P('blk', 'narrow')
- cross: float32 [64, 2, 256], P(('blk', 'narrow'))
Inputs may be any that keep to these rules, and one draw needn't show every extreme that they name: `col_index`: each block column index differs from its own block row by 1 or 2 in either direction, near the ends of the range reflected to the other side; the three indices of a row may repeat.
All inputs are finite; a program needn't handle non-finite values.
Results may differ from a plain program's by a relative error of at most 0.0001.
Values sent between devices are 32-bit elements; how exact they have to be, the bound alone decides.
A program may use at most 64 MiB of HBM per device.

v0:
```python
import jax
import jax.numpy as jnp
from jax import lax
from jax.sharding import PartitionSpec as P

SWEEPS = 8
precise = lax.Precision.HIGHEST


def extended_2(cells, sides, width):
    for axis, dim in sides:
        count = lax.axis_size(axis)
        ends = count - 1
        head = lax.slice_in_dim(cells, 0, width, axis=dim)
        tail = lax.slice_in_dim(cells, cells.shape[dim] - width, cells.shape[dim], axis=dim)
        cells = jnp.concatenate(
            [
                lax.ppermute(tail, axis, [(i, (i + 1) % count) for i in range(ends)]),
                cells,
                lax.ppermute(head, axis, [((i + 1) % count, i) for i in range(ends)]),
            ],
            axis=dim,
        )
    return cells


def block_product(matrices, field):
    return jnp.einsum("nab,nbk->nak", matrices, field, precision=precise)


def shards(rhs, zo, e_diag, a_off, e_off, col_index, inv_diag, shifts):
    row_count, col_width = rhs.shape
    blocks = e_diag.shape[0]
    block_size = e_diag.shape[1]
    local_col = col_index - lax.axis_index("blk") * blocks + 2

    def coupled(coupling, field):
        padded = extended_2(field.reshape(row_count, col_width), (("blk", 0),), 2 * block_size)
        extended = padded.reshape(blocks + 4, block_size, col_width)
        picked = jnp.take(extended, local_col, axis=0)
        return jnp.einsum("nsab,nsbk->nak", coupling, picked, precision=precise)

    current = rhs.reshape(blocks, block_size, col_width)
    images = []
    for which in range(2):
        shift_value = shifts[which]
        coupling = a_off - shift_value * e_off
        inverse = inv_diag[which]
        iterate = block_product(inverse, current)
        for sweep in range(SWEEPS):
            iterate = block_product(inverse, current - coupled(coupling, iterate))
        mass_image = block_product(e_diag, iterate) + coupled(e_off, iterate)
        current = current + 2.0 * shift_value * mass_image
        images.append(jnp.sqrt(2.0 * shift_value) * mass_image)
    stacked = jnp.stack(images, axis=2).reshape(row_count, 2, col_width)
    summed = lax.psum_scatter(
        jnp.einsum("ro,rsk->osk", zo, stacked, precision=precise),
        "blk",
        scatter_dimension=0,
        tiled=True,
    )
    cross = lax.all_to_all(summed, "narrow", split_axis=0, concat_axis=2, tiled=True)
    return (current.reshape(row_count, col_width), cross)


def solution(mesh):
    placed = (
        P("blk", "narrow"),
        P("blk", None),
        P("blk", None, None),
        P("blk", None, None, None),
        P("blk", None, None, None),
        P("blk", None),
        P(None, "blk", None, None),
        P(),
    )
    return jax.shard_map(
        shards,
        mesh=mesh,
        in_specs=placed,
        out_specs=(P("blk", "narrow"), P(("blk", "narrow"), None, None)),
        check_vma=False,
    )
```

profile of v0, /device:TPU:8, one launch (start us, length us, event | category | flops | bytes accessed | tf_op | source)
XLA Modules:
  0.0 328.5 jit_solution(1364033609867359985)
XLA Ops:
  10.6 4.5 %collective-permute-start.1 = (f32[192,128]{1,0:T(8,128)S(1)}, f32[192,128]{1,0:T(8,128)S(1)}, u32[]{:S(2)}, u32[]{:S(2)}) collective-permute-start(f32[192,128]{1,0:T(8,128)S(1)} %bitcast.399), channel_id=1, source_target_pairs={{2,0},{4,2},{6,4},{8,6},{10,8},{12,10},{14,12},{16,14},{18,16},{20... | collective-permute-start | bytes 294920 | tf_op jit(solution)/shard_map/ppermute | solution.py:20
  25.3 4.5 %collective-permute-start.3 = (f32[192,128]{1,0:T(8,128)S(1)}, f32[192,128]{1,0:T(8,128)S(1)}, u32[]{:S(2)}, u32[]{:S(2)}) collective-permute-start(f32[192,128]{1,0:T(8,128)S(1)} %bitcast.406), channel_id=1, source_target_pairs={{2,0},{4,2},{6,4},{8,6},{10,8},{12,10},{14,12},{16,14},{18,16},{20... | collective-permute-start | bytes 294920 | tf_op jit(solution)/shard_map/ppermute | solution.py:20
  36.9 4.6 %collective-permute-start.5 = (f32[192,128]{1,0:T(8,128)S(1)}, f32[192,128]{1,0:T(8,128)S(1)}, u32[]{:S(2)}, u32[]{:S(2)}) collective-permute-start(f32[192,128]{1,0:T(8,128)S(1)} %bitcast.407), channel_id=1, source_target_pairs={{2,0},{4,2},{6,4},{8,6},{10,8},{12,10},{14,12},{16,14},{18,16},{20... | collective-permute-start | bytes 294920 | tf_op jit(solution)/shard_map/ppermute | solution.py:20
  46.7 2.6 collective-permute-start.6
  49.3 3.9 %collective-permute-start.7 = (f32[192,128]{1,0:T(8,128)S(1)}, f32[192,128]{1,0:T(8,128)S(1)}, u32[]{:S(2)}, u32[]{:S(2)}) collective-permute-start(f32[192,128]{1,0:T(8,128)S(1)} %bitcast.408), channel_id=1, source_target_pairs={{2,0},{4,2},{6,4},{8,6},{10,8},{12,10},{14,12},{16,14},{18,16},{20... | collective-permute-start | bytes 294920 | tf_op jit(solution)/shard_map/ppermute | solution.py:20
  61.0 4.0 %collective-permute-start.9 = (f32[192,128]{1,0:T(8,128)S(1)}, f32[192,128]{1,0:T(8,128)S(1)}, u32[]{:S(2)}, u32[]{:S(2)}) collective-permute-start(f32[192,128]{1,0:T(8,128)S(1)} %bitcast.409), channel_id=1, source_target_pairs={{2,0},{4,2},{6,4},{8,6},{10,8},{12,10},{14,12},{16,14},{18,16},{20... | collective-permute-start | bytes 294920 | tf_op jit(solution)/shard_map/ppermute | solution.py:20
  72.8 3.9 %collective-permute-start.11 = (f32[192,128]{1,0:T(8,128)S(1)}, f32[192,128]{1,0:T(8,128)S(1)}, u32[]{:S(2)}, u32[]{:S(2)}) collective-permute-start(f32[192,128]{1,0:T(8,128)S(1)} %bitcast.410), channel_id=1, source_target_pairs={{2,0},{4,2},{6,4},{8,6},{10,8},{12,10},{14,12},{16,14},{18,16},{20... | collective-permute-start | bytes 294920 | tf_op jit(solution)/shard_map/ppermute | solution.py:20
  81.9 2.6 collective-permute-start.12
  84.5 4.0 %collective-permute-start.13 = (f32[192,128]{1,0:T(8,128)S(1)}, f32[192,128]{1,0:T(8,128)S(1)}, u32[]{:S(2)}, u32[]{:S(2)}) collective-permute-start(f32[192,128]{1,0:T(8,128)S(1)} %bitcast.411), channel_id=1, source_target_pairs={{2,0},{4,2},{6,4},{8,6},{10,8},{12,10},{14,12},{16,14},{18,16},{20... | collective-permute-start | bytes 294920 | tf_op jit(solution)/shard_map/ppermute | solution.py:20
  96.2 4.1 %collective-permute-start.15 = (f32[192,128]{1,0:T(8,128)S(1)}, f32[192,128]{1,0:T(8,128)S(1)}, u32[]{:S(2)}, u32[]{:S(2)}) collective-permute-start(f32[192,128]{1,0:T(8,128)S(1)} %bitcast.412), channel_id=1, source_target_pairs={{2,0},{4,2},{6,4},{8,6},{10,8},{12,10},{14,12},{16,14},{18,16},{20... | collective-permute-start | bytes 294920 | tf_op jit(solution)/shard_map/ppermute | solution.py:20
  105.4 2.6 collective-permute-start.16
  108.0 3.9 %collective-permute-start.17 = (f32[192,128]{1,0:T(8,128)S(1)}, f32[192,128]{1,0:T(8,128)S(1)}, u32[]{:S(2)}, u32[]{:S(2)}) collective-permute-start(f32[192,128]{1,0:T(8,128)S(1)} %bitcast.404), channel_id=1, source_target_pairs={{2,0},{4,2},{6,4},{8,6},{10,8},{12,10},{14,12},{16,14},{18,16},{20... | collective-permute-start | bytes 294920 | tf_op jit(solution)/shard_map/ppermute | solution.py:20
  117.7 2.6 collective-permute-start.18
  120.3 3.9 %collective-permute-start.19 = (f32[192,128]{1,0:T(8,128)S(1)}, f32[192,128]{1,0:T(8,128)S(1)}, u32[]{:S(2)}, u32[]{:S(2)}) collective-permute-start(f32[192,128]{1,0:T(8,128)S(1)} %bitcast.413), channel_id=1, source_target_pairs={{2,0},{4,2},{6,4},{8,6},{10,8},{12,10},{14,12},{16,14},{18,16},{20... | collective-permute-start | bytes 294920 | tf_op jit(solution)/shard_map/ppermute | solution.py:20
  129.3 2.6 collective-permute-start.20
  132.0 3.9 %collective-permute-start.21 = (f32[192,128]{1,0:T(8,128)S(1)}, f32[192,128]{1,0:T(8,128)S(1)}, u32[]{:S(2)}, u32[]{:S(2)}) collective-permute-start(f32[192,128]{1,0:T(8,128)S(1)} %bitcast.414), channel_id=1, source_target_pairs={{2,0},{4,2},{6,4},{8,6},{10,8},{12,10},{14,12},{16,14},{18,16},{20... | collective-permute-start | bytes 294920 | tf_op jit(solution)/shard_map/ppermute | solution.py:20
  141.1 2.6 collective-permute-start.22
  143.7 3.9 %collective-permute-start.23 = (f32[192,128]{1,0:T(8,128)S(1)}, f32[192,128]{1,0:T(8,128)S(1)}, u32[]{:S(2)}, u32[]{:S(2)}) collective-permute-start(f32[192,128]{1,0:T(8,128)S(1)} %bitcast.415), channel_id=1, source_target_pairs={{2,0},{4,2},{6,4},{8,6},{10,8},{12,10},{14,12},{16,14},{18,16},{20... | collective-permute-start | bytes 294920 | tf_op jit(solution)/shard_map/ppermute | solution.py:20
  152.8 2.6 collective-permute-start.24
  155.4 3.9 %collective-permute-start.25 = (f32[192,128]{1,0:T(8,128)S(1)}, f32[192,128]{1,0:T(8,128)S(1)}, u32[]{:S(2)}, u32[]{:S(2)}) collective-permute-start(f32[192,128]{1,0:T(8,128)S(1)} %bitcast.416), channel_id=1, source_target_pairs={{2,0},{4,2},{6,4},{8,6},{10,8},{12,10},{14,12},{16,14},{18,16},{20... | collective-permute-start | bytes 294920 | tf_op jit(solution)/shard_map/ppermute | solution.py:20
  164.5 2.6 collective-permute-start.26
  167.2 3.9 %collective-permute-start.27 = (f32[192,128]{1,0:T(8,128)S(1)}, f32[192,128]{1,0:T(8,128)S(1)}, u32[]{:S(2)}, u32[]{:S(2)}) collective-permute-start(f32[192,128]{1,0:T(8,128)S(1)} %bitcast.417), channel_id=1, source_target_pairs={{2,0},{4,2},{6,4},{8,6},{10,8},{12,10},{14,12},{16,14},{18,16},{20... | collective-permute-start | bytes 294920 | tf_op jit(solution)/shard_map/ppermute | solution.py:20
  176.3 2.6 collective-permute-start.28
  178.9 3.9 %collective-permute-start.29 = (f32[192,128]{1,0:T(8,128)S(1)}, f32[192,128]{1,0:T(8,128)S(1)}, u32[]{:S(2)}, u32[]{:S(2)}) collective-permute-start(f32[192,128]{1,0:T(8,128)S(1)} %bitcast.418), channel_id=1, source_target_pairs={{2,0},{4,2},{6,4},{8,6},{10,8},{12,10},{14,12},{16,14},{18,16},{20... | collective-permute-start | bytes 294920 | tf_op jit(solution)/shard_map/ppermute | solution.py:20
  188.0 2.6 collective-permute-start.30
  190.6 4.2 %collective-permute-start.31 = (f32[192,128]{1,0:T(8,128)S(1)}, f32[192,128]{1,0:T(8,128)S(1)}, u32[]{:S(2)}, u32[]{:S(2)}) collective-permute-start(f32[192,128]{1,0:T(8,128)S(1)} %bitcast.419), channel_id=1, source_target_pairs={{2,0},{4,2},{6,4},{8,6},{10,8},{12,10},{14,12},{16,14},{18,16},{20... | collective-permute-start | bytes 294920 | tf_op jit(solution)/shard_map/ppermute | solution.py:20
  199.7 2.6 collective-permute-start.32
  202.3 3.9 %collective-permute-start.33 = (f32[192,128]{1,0:T(8,128)S(1)}, f32[192,128]{1,0:T(8,128)S(1)}, u32[]{:S(2)}, u32[]{:S(2)}) collective-permute-start(f32[192,128]{1,0:T(8,128)S(1)} %bitcast.401), channel_id=1, source_target_pairs={{2,0},{4,2},{6,4},{8,6},{10,8},{12,10},{14,12},{16,14},{18,16},{20... | collective-permute-start | bytes 294920 | tf_op jit(solution)/shard_map/ppermute | solution.py:20
  210.4 2.6 collective-permute-start.34
  213.0 3.9 %collective-permute-start.35 = (f32[192,128]{1,0:T(8,128)S(1)}, f32[192,128]{1,0:T(8,128)S(1)}, u32[]{:S(2)}, u32[]{:S(2)}) collective-permute-start(f32[192,128]{1,0:T(8,128)S(1)} %bitcast.402), channel_id=1, source_target_pairs={{2,0},{4,2},{6,4},{8,6},{10,8},{12,10},{14,12},{16,14},{18,16},{20... | collective-permute-start | bytes 294920 | tf_op jit(solution)/shard_map/ppermute | solution.py:20
  225.6 88.5 %all-reduce.3.cloned.1.call-done = f32[64,2,128]{2,0,1:T(8,128)} async-done(((f32[64,2,128]{2,0,1:T(8,128)}), f32[64,2,128]{2,0,1:T(8,128)}) %all-reduce.3.cloned.1.call-update) | async-done | bytes 65552
  314.7 6.3 %all_to_all.18 = f32[4,2,128]{2,1,0:T(2,128)S(1)} all-to-all(f32[4,2,128]{2,1,0:T(2,128)S(1)} %copy.11), channel_id=1, replica_groups=mesh['blk'=16,'narrow'=2] {'narrow'}, dimensions={0} | all-to-all | bytes 8192 | tf_op jit(solution)/shard_map/all_to_all | solution.py:62
  (168 shorter events, 112.0 us)
Async XLA Ops:
  7.2 306.8 %all-reduce.3.cloned.1.call-start = ((), (), s32[]{:S(2)}) async-start(), calls=%async_computation.1 | async-start | bytes 131072
  8.7 10.9 %collective-permute-start = (f32[192,128]{1,0:T(8,128)S(1)}, f32[192,128]{1,0:T(8,128)S(1)}, u32[]{:S(2)}, u32[]{:S(2)}) collective-permute-start(f32[192,128]{1,0:T(8,128)S(1)} %bitcast.400), channel_id=1, source_target_pairs={{0,2},{2,4},{4,6},{6,8},{8,10},{10,12},{12,14},{14,16},{16,18},{18... | collective-permute-start | bytes 294920 | tf_op jit(solution)/shard_map/ppermute | solution.py:18
  10.6 9.0 %collective-permute-start.1 = (f32[192,128]{1,0:T(8,128)S(1)}, f32[192,128]{1,0:T(8,128)S(1)}, u32[]{:S(2)}, u32[]{:S(2)}) collective-permute-start(f32[192,128]{1,0:T(8,128)S(1)} %bitcast.399), channel_id=1, source_target_pairs={{2,0},{4,2},{6,4},{8,6},{10,8},{12,10},{14,12},{16,14},{18,16},{20... | collective-permute-start | bytes 294920 | tf_op jit(solution)/shard_map/ppermute | solution.py:20
  23.3 6.8 %collective-permute-start.2 = (f32[192,128]{1,0:T(8,128)S(1)}, f32[192,128]{1,0:T(8,128)S(1)}, u32[]{:S(2)}, u32[]{:S(2)}) collective-permute-start(f32[192,128]{1,0:T(8,128)S(1)} %bitcast.421), channel_id=1, source_target_pairs={{0,2},{2,4},{4,6},{6,8},{8,10},{10,12},{12,14},{14,16},{16,18},{18... | collective-permute-start | bytes 294920 | tf_op jit(solution)/shard_map/ppermute | solution.py:18
  25.3 6.7 %collective-permute-start.3 = (f32[192,128]{1,0:T(8,128)S(1)}, f32[192,128]{1,0:T(8,128)S(1)}, u32[]{:S(2)}, u32[]{:S(2)}) collective-permute-start(f32[192,128]{1,0:T(8,128)S(1)} %bitcast.406), channel_id=1, source_target_pairs={{2,0},{4,2},{6,4},{8,6},{10,8},{12,10},{14,12},{16,14},{18,16},{20... | collective-permute-start | bytes 294920 | tf_op jit(solution)/shard_map/ppermute | solution.py:20
  35.0 6.9 %collective-permute-start.4 = (f32[192,128]{1,0:T(8,128)S(1)}, f32[192,128]{1,0:T(8,128)S(1)}, u32[]{:S(2)}, u32[]{:S(2)}) collective-permute-start(f32[192,128]{1,0:T(8,128)S(1)} %bitcast.422), channel_id=1, source_target_pairs={{0,2},{2,4},{4,6},{6,8},{8,10},{10,12},{12,14},{14,16},{16,18},{18... | collective-permute-start | bytes 294920 | tf_op jit(solution)/shard_map/ppermute | solution.py:18
  36.9 6.8 %collective-permute-start.5 = (f32[192,128]{1,0:T(8,128)S(1)}, f32[192,128]{1,0:T(8,128)S(1)}, u32[]{:S(2)}, u32[]{:S(2)}) collective-permute-start(f32[192,128]{1,0:T(8,128)S(1)} %bitcast.407), channel_id=1, source_target_pairs={{2,0},{4,2},{6,4},{8,6},{10,8},{12,10},{14,12},{16,14},{18,16},{20... | collective-permute-start | bytes 294920 | tf_op jit(solution)/shard_map/ppermute | solution.py:20
  46.7 6.9 %collective-permute-start.6 = (f32[192,128]{1,0:T(8,128)S(1)}, f32[192,128]{1,0:T(8,128)S(1)}, u32[]{:S(2)}, u32[]{:S(2)}) collective-permute-start(f32[192,128]{1,0:T(8,128)S(1)} %bitcast.423), channel_id=1, source_target_pairs={{0,2},{2,4},{4,6},{6,8},{8,10},{10,12},{12,14},{14,16},{16,18},{18... | collective-permute-start | bytes 294920 | tf_op jit(solution)/shard_map/ppermute | solution.py:18
  49.3 6.1 %collective-permute-start.7 = (f32[192,128]{1,0:T(8,128)S(1)}, f32[192,128]{1,0:T(8,128)S(1)}, u32[]{:S(2)}, u32[]{:S(2)}) collective-permute-start(f32[192,128]{1,0:T(8,128)S(1)} %bitcast.408), channel_id=1, source_target_pairs={{2,0},{4,2},{6,4},{8,6},{10,8},{12,10},{14,12},{16,14},{18,16},{20... | collective-permute-start | bytes 294920 | tf_op jit(solution)/shard_map/ppermute | solution.py:20
  58.4 6.9 %collective-permute-start.8 = (f32[192,128]{1,0:T(8,128)S(1)}, f32[192,128]{1,0:T(8,128)S(1)}, u32[]{:S(2)}, u32[]{:S(2)}) collective-permute-start(f32[192,128]{1,0:T(8,128)S(1)} %bitcast.424), channel_id=1, source_target_pairs={{0,2},{2,4},{4,6},{6,8},{8,10},{10,12},{12,14},{14,16},{16,18},{18... | collective-permute-start | bytes 294920 | tf_op jit(solution)/shard_map/ppermute | solution.py:18
  61.0 6.2 %collective-permute-start.9 = (f32[192,128]{1,0:T(8,128)S(1)}, f32[192,128]{1,0:T(8,128)S(1)}, u32[]{:S(2)}, u32[]{:S(2)}) collective-permute-start(f32[192,128]{1,0:T(8,128)S(1)} %bitcast.409), channel_id=1, source_target_pairs={{2,0},{4,2},{6,4},{8,6},{10,8},{12,10},{14,12},{16,14},{18,16},{20... | collective-permute-start | bytes 294920 | tf_op jit(solution)/shard_map/ppermute | solution.py:20
  70.2 6.9 %collective-permute-start.10 = (f32[192,128]{1,0:T(8,128)S(1)}, f32[192,128]{1,0:T(8,128)S(1)}, u32[]{:S(2)}, u32[]{:S(2)}) collective-permute-start(f32[192,128]{1,0:T(8,128)S(1)} %bitcast.425), channel_id=1, source_target_pairs={{0,2},{2,4},{4,6},{6,8},{8,10},{10,12},{12,14},{14,16},{16,18},{18... | collective-permute-start | bytes 294920 | tf_op jit(solution)/shard_map/ppermute | solution.py:18
  72.8 6.1 %collective-permute-start.11 = (f32[192,128]{1,0:T(8,128)S(1)}, f32[192,128]{1,0:T(8,128)S(1)}, u32[]{:S(2)}, u32[]{:S(2)}) collective-permute-start(f32[192,128]{1,0:T(8,128)S(1)} %bitcast.410), channel_id=1, source_target_pairs={{2,0},{4,2},{6,4},{8,6},{10,8},{12,10},{14,12},{16,14},{18,16},{20... | collective-permute-start | bytes 294920 | tf_op jit(solution)/shard_map/ppermute | solution.py:20
  81.9 6.9 %collective-permute-start.12 = (f32[192,128]{1,0:T(8,128)S(1)}, f32[192,128]{1,0:T(8,128)S(1)}, u32[]{:S(2)}, u32[]{:S(2)}) collective-permute-start(f32[192,128]{1,0:T(8,128)S(1)} %bitcast.426), channel_id=1, source_target_pairs={{0,2},{2,4},{4,6},{6,8},{8,10},{10,12},{12,14},{14,16},{16,18},{18... | collective-permute-start | bytes 294920 | tf_op jit(solution)/shard_map/ppermute | solution.py:18
  84.5 6.2 %collective-permute-start.13 = (f32[192,128]{1,0:T(8,128)S(1)}, f32[192,128]{1,0:T(8,128)S(1)}, u32[]{:S(2)}, u32[]{:S(2)}) collective-permute-start(f32[192,128]{1,0:T(8,128)S(1)} %bitcast.411), channel_id=1, source_target_pairs={{2,0},{4,2},{6,4},{8,6},{10,8},{12,10},{14,12},{16,14},{18,16},{20... | collective-permute-start | bytes 294920 | tf_op jit(solution)/shard_map/ppermute | solution.py:20
  93.6 6.9 %collective-permute-start.14 = (f32[192,128]{1,0:T(8,128)S(1)}, f32[192,128]{1,0:T(8,128)S(1)}, u32[]{:S(2)}, u32[]{:S(2)}) collective-permute-start(f32[192,128]{1,0:T(8,128)S(1)} %bitcast.427), channel_id=1, source_target_pairs={{0,2},{2,4},{4,6},{6,8},{8,10},{10,12},{12,14},{14,16},{16,18},{18... | collective-permute-start | bytes 294920 | tf_op jit(solution)/shard_map/ppermute | solution.py:18
  96.2 6.1 %collective-permute-start.15 = (f32[192,128]{1,0:T(8,128)S(1)}, f32[192,128]{1,0:T(8,128)S(1)}, u32[]{:S(2)}, u32[]{:S(2)}) collective-permute-start(f32[192,128]{1,0:T(8,128)S(1)} %bitcast.412), channel_id=1, source_target_pairs={{2,0},{4,2},{6,4},{8,6},{10,8},{12,10},{14,12},{16,14},{18,16},{20... | collective-permute-start | bytes 294920 | tf_op jit(solution)/shard_map/ppermute | solution.py:20
  105.4 7.2 %collective-permute-start.16 = (f32[192,128]{1,0:T(8,128)S(1)}, f32[192,128]{1,0:T(8,128)S(1)}, u32[]{:S(2)}, u32[]{:S(2)}) collective-permute-start(f32[192,128]{1,0:T(8,128)S(1)} %bitcast.420), channel_id=1, source_target_pairs={{0,2},{2,4},{4,6},{6,8},{8,10},{10,12},{12,14},{14,16},{16,18},{18... | collective-permute-start | bytes 294920 | tf_op jit(solution)/shard_map/ppermute | solution.py:18
  108.0 6.1 %collective-permute-start.17 = (f32[192,128]{1,0:T(8,128)S(1)}, f32[192,128]{1,0:T(8,128)S(1)}, u32[]{:S(2)}, u32[]{:S(2)}) collective-permute-start(f32[192,128]{1,0:T(8,128)S(1)} %bitcast.404), channel_id=1, source_target_pairs={{2,0},{4,2},{6,4},{8,6},{10,8},{12,10},{14,12},{16,14},{18,16},{20... | collective-permute-start | bytes 294920 | tf_op jit(solution)/shard_map/ppermute | solution.py:20
  117.7 6.9 %collective-permute-start.18 = (f32[192,128]{1,0:T(8,128)S(1)}, f32[192,128]{1,0:T(8,128)S(1)}, u32[]{:S(2)}, u32[]{:S(2)}) collective-permute-start(f32[192,128]{1,0:T(8,128)S(1)} %bitcast.428), channel_id=1, source_target_pairs={{0,2},{2,4},{4,6},{6,8},{8,10},{10,12},{12,14},{14,16},{16,18},{18... | collective-permute-start | bytes 294920 | tf_op jit(solution)/shard_map/ppermute | solution.py:18
  120.3 6.1 %collective-permute-start.19 = (f32[192,128]{1,0:T(8,128)S(1)}, f32[192,128]{1,0:T(8,128)S(1)}, u32[]{:S(2)}, u32[]{:S(2)}) collective-permute-start(f32[192,128]{1,0:T(8,128)S(1)} %bitcast.413), channel_id=1, source_target_pairs={{2,0},{4,2},{6,4},{8,6},{10,8},{12,10},{14,12},{16,14},{18,16},{20... | collective-permute-start | bytes 294920 | tf_op jit(solution)/shard_map/ppermute | solution.py:20
  129.3 6.9 %collective-permute-start.20 = (f32[192,128]{1,0:T(8,128)S(1)}, f32[192,128]{1,0:T(8,128)S(1)}, u32[]{:S(2)}, u32[]{:S(2)}) collective-permute-start(f32[192,128]{1,0:T(8,128)S(1)} %bitcast.429), channel_id=1, source_target_pairs={{0,2},{2,4},{4,6},{6,8},{8,10},{10,12},{12,14},{14,16},{16,18},{18... | collective-permute-start | bytes 294920 | tf_op jit(solution)/shard_map/ppermute | solution.py:18
  132.0 6.1 %collective-permute-start.21 = (f32[192,128]{1,0:T(8,128)S(1)}, f32[192,128]{1,0:T(8,128)S(1)}, u32[]{:S(2)}, u32[]{:S(2)}) collective-permute-start(f32[192,128]{1,0:T(8,128)S(1)} %bitcast.414), channel_id=1, source_target_pairs={{2,0},{4,2},{6,4},{8,6},{10,8},{12,10},{14,12},{16,14},{18,16},{20... | collective-permute-start | bytes 294920 | tf_op jit(solution)/shard_map/ppermute | solution.py:20
  141.1 6.9 %collective-permute-start.22 = (f32[192,128]{1,0:T(8,128)S(1)}, f32[192,128]{1,0:T(8,128)S(1)}, u32[]{:S(2)}, u32[]{:S(2)}) collective-permute-start(f32[192,128]{1,0:T(8,128)S(1)} %bitcast.430), channel_id=1, source_target_pairs={{0,2},{2,4},{4,6},{6,8},{8,10},{10,12},{12,14},{14,16},{16,18},{18... | collective-permute-start | bytes 294920 | tf_op jit(solution)/shard_map/ppermute | solution.py:18
  152.8 6.9 %collective-permute-start.24 = (f32[192,128]{1,0:T(8,128)S(1)}, f32[192,128]{1,0:T(8,128)S(1)}, u32[]{:S(2)}, u32[]{:S(2)}) collective-permute-start(f32[192,128]{1,0:T(8,128)S(1)} %bitcast.431), channel_id=1, source_target_pairs={{0,2},{2,4},{4,6},{6,8},{8,10},{10,12},{12,14},{14,16},{16,18},{18... | collective-permute-start | bytes 294920 | tf_op jit(solution)/shard_map/ppermute | solution.py:18
  155.4 6.1 %collective-permute-start.25 = (f32[192,128]{1,0:T(8,128)S(1)}, f32[192,128]{1,0:T(8,128)S(1)}, u32[]{:S(2)}, u32[]{:S(2)}) collective-permute-start(f32[192,128]{1,0:T(8,128)S(1)} %bitcast.416), channel_id=1, source_target_pairs={{2,0},{4,2},{6,4},{8,6},{10,8},{12,10},{14,12},{16,14},{18,16},{20... | collective-permute-start | bytes 294920 | tf_op jit(solution)/shard_map/ppermute | solution.py:20
  164.5 6.9 %collective-permute-start.26 = (f32[192,128]{1,0:T(8,128)S(1)}, f32[192,128]{1,0:T(8,128)S(1)}, u32[]{:S(2)}, u32[]{:S(2)}) collective-permute-start(f32[192,128]{1,0:T(8,128)S(1)} %bitcast.432), channel_id=1, source_target_pairs={{0,2},{2,4},{4,6},{6,8},{8,10},{10,12},{12,14},{14,16},{16,18},{18... | collective-permute-start | bytes 294920 | tf_op jit(solution)/shard_map/ppermute | solution.py:18
  176.3 6.9 %collective-permute-start.28 = (f32[192,128]{1,0:T(8,128)S(1)}, f32[192,128]{1,0:T(8,128)S(1)}, u32[]{:S(2)}, u32[]{:S(2)}) collective-permute-start(f32[192,128]{1,0:T(8,128)S(1)} %bitcast.433), channel_id=1, source_target_pairs={{0,2},{2,4},{4,6},{6,8},{8,10},{10,12},{12,14},{14,16},{16,18},{18... | collective-permute-start | bytes 294920 | tf_op jit(solution)/shard_map/ppermute | solution.py:18
  188.0 6.9 %collective-permute-start.30 = (f32[192,128]{1,0:T(8,128)S(1)}, f32[192,128]{1,0:T(8,128)S(1)}, u32[]{:S(2)}, u32[]{:S(2)}) collective-permute-start(f32[192,128]{1,0:T(8,128)S(1)} %bitcast.434), channel_id=1, source_target_pairs={{0,2},{2,4},{4,6},{6,8},{8,10},{10,12},{12,14},{14,16},{16,18},{18... | collective-permute-start | bytes 294920 | tf_op jit(solution)/shard_map/ppermute | solution.py:18
  199.7 7.3 %collective-permute-start.32 = (f32[192,128]{1,0:T(8,128)S(1)}, f32[192,128]{1,0:T(8,128)S(1)}, u32[]{:S(2)}, u32[]{:S(2)}) collective-permute-start(f32[192,128]{1,0:T(8,128)S(1)} %bitcast.403), channel_id=1, source_target_pairs={{0,2},{2,4},{4,6},{6,8},{8,10},{10,12},{12,14},{14,16},{16,18},{18... | collective-permute-start | bytes 294920 | tf_op jit(solution)/shard_map/ppermute | solution.py:18
  210.4 6.9 %collective-permute-start.34 = (f32[192,128]{1,0:T(8,128)S(1)}, f32[192,128]{1,0:T(8,128)S(1)}, u32[]{:S(2)}, u32[]{:S(2)}) collective-permute-start(f32[192,128]{1,0:T(8,128)S(1)} %bitcast.405), channel_id=1, source_target_pairs={{0,2},{2,4},{4,6},{6,8},{8,10},{10,12},{12,14},{14,16},{16,18},{18... | collective-permute-start | bytes 294920 | tf_op jit(solution)/shard_map/ppermute | solution.py:18
  213.0 6.1 %collective-permute-start.35 = (f32[192,128]{1,0:T(8,128)S(1)}, f32[192,128]{1,0:T(8,128)S(1)}, u32[]{:S(2)}, u32[]{:S(2)}) collective-permute-start(f32[192,128]{1,0:T(8,128)S(1)} %bitcast.402), channel_id=1, source_target_pairs={{2,0},{4,2},{6,4},{8,6},{10,8},{12,10},{14,12},{16,14},{18,16},{20... | collective-permute-start | bytes 294920 | tf_op jit(solution)/shard_map/ppermute | solution.py:20
  (15 other events, 155.9 us)
Sparse Core Ops, SparseCore 0:
  223.8 90.1 all-reduce.2
where the time goes:
time: 330 us; the launch traced here: 329 us
  waiting for transfers between devices  124 us (38%)
  starting transfers between devices  118 us (36%)
  matrix products  39.9 us (12%)
  local copies, waits for them, and re-layouts  19.9 us (6%)
  between operations  17.1 us (5%)
  blocking collectives  6.32 us (2%)
    unnamed x2, waiting for transfers between devices  88.5 us
    ppermute x18, starting transfers between devices, extended_2(): lax.ppermute(head, axis, [((i + 1) % count, i) for i in range(ends)])  73.3 us
    ppermute x18, starting transfers between devices, extended_2(): lax.ppermute(tail, axis, [(i, (i + 1) % count) for i in range(ends)])  44.9 us
    ppermute x18, waiting for transfers between devices, extended_2(): lax.ppermute(head, axis, [((i + 1) % count, i) for i in range(ends)])  30.5 us
    dot_general x20, matrix products, block_product(): return jnp.einsum('nab,nbk->nak', matrices, field, precision=precise)  22.2 us
    dot_general x18, matrix products, coupled(): return jnp.einsum('nsab,nsbk->nak', coupling, picked, precision=precise)  16.8 us
    gather x18, local copies, waits for them, and re-layouts, coupled(): picked = jnp.take(extended, local_col, axis=0)  12.2 us
  transfers between devices with their start and end apart: 37, of which 33 were waited for; matrix products, arithmetic and copies ran while one was open for 1% of the time, Pallas kernels for 0%

commit v1 on v0

--- a/solution.py
+++ b/solution.py
@@ -59,7 +59,12 @@
         scatter_dimension=0,
         tiled=True,
     )
-    cross = lax.all_to_all(summed, "narrow", split_axis=0, concat_axis=2, tiled=True)
+    cross = jnp.concatenate(
+        lax.all_to_all(
+            jnp.stack(jnp.split(summed, lax.axis_size("narrow"), axis=0)), "narrow", 0, 0
+        ),
+        axis=2,
+    )
     return (current.reshape(row_count, col_width), cross)
 
 

time: 330 us -> 331 us (level)
  no operation moved by 1% of the time
where the time goes in v1:
time: 331 us; the launch traced here: 329 us
  waiting for transfers between devices  124 us (37%)
  starting transfers between devices  118 us (36%)
  matrix products  40.1 us (12%)
  local copies, waits for them, and re-layouts  20 us (6%)
  between operations  17.1 us (5%)
  blocking collectives  6.33 us (2%)
    unnamed x2, waiting for transfers between devices  88.6 us
    ppermute x18, starting transfers between devices, extended_2(): lax.ppermute(head, axis, [((i + 1) % count, i) for i in range(ends)])  73.1 us
    ppermute x18, starting transfers between devices, extended_2(): lax.ppermute(tail, axis, [(i, (i + 1) % count) for i in range(ends)])  45.1 us
    ppermute x18, waiting for transfers between devices, extended_2(): lax.ppermute(head, axis, [((i + 1) % count, i) for i in range(ends)])  30.5 us
    dot_general x20, matrix products, block_product(): return jnp.einsum('nab,nbk->nak', matrices, field, precision=precise)  22.2 us
    dot_general x18, matrix products, coupled(): return jnp.einsum('nsab,nsbk->nak', coupling, picked, precision=precise)  16.9 us
    gather x18, local copies, waits for them, and re-layouts, coupled(): picked = jnp.take(extended, local_col, axis=0)  12.2 us
  transfers between devices with their start and end apart: 37, of which 33 were waited for; matrix products, arithmetic and copies ran while one was open for 1% of the time, Pallas kernels for 0%

profile of v1, /device:TPU:8, one launch (start us, length us, event | category | flops | bytes accessed | tf_op | source)
XLA Modules:
  0.0 328.9 jit_solution(14300190164345001334)
XLA Ops:
  10.6 4.5 %collective-permute-start.1 = (f32[192,128]{1,0:T(8,128)S(1)}, f32[192,128]{1,0:T(8,128)S(1)}, u32[]{:S(2)}, u32[]{:S(2)}) collective-permute-start(f32[192,128]{1,0:T(8,128)S(1)} %bitcast.397), channel_id=1, source_target_pairs={{2,0},{4,2},{6,4},{8,6},{10,8},{12,10},{14,12},{16,14},{18,16},{20... | collective-permute-start | bytes 294920 | tf_op jit(solution)/shard_map/ppermute | solution.py:20
  25.3 4.5 %collective-permute-start.3 = (f32[192,128]{1,0:T(8,128)S(1)}, f32[192,128]{1,0:T(8,128)S(1)}, u32[]{:S(2)}, u32[]{:S(2)}) collective-permute-start(f32[192,128]{1,0:T(8,128)S(1)} %bitcast.404), channel_id=1, source_target_pairs={{2,0},{4,2},{6,4},{8,6},{10,8},{12,10},{14,12},{16,14},{18,16},{20... | collective-permute-start | bytes 294920 | tf_op jit(solution)/shard_map/ppermute | solution.py:20
  36.9 4.6 %collective-permute-start.5 = (f32[192,128]{1,0:T(8,128)S(1)}, f32[192,128]{1,0:T(8,128)S(1)}, u32[]{:S(2)}, u32[]{:S(2)}) collective-permute-start(f32[192,128]{1,0:T(8,128)S(1)} %bitcast.405), channel_id=1, source_target_pairs={{2,0},{4,2},{6,4},{8,6},{10,8},{12,10},{14,12},{16,14},{18,16},{20... | collective-permute-start | bytes 294920 | tf_op jit(solution)/shard_map/ppermute | solution.py:20
  49.4 3.9 %collective-permute-start.7 = (f32[192,128]{1,0:T(8,128)S(1)}, f32[192,128]{1,0:T(8,128)S(1)}, u32[]{:S(2)}, u32[]{:S(2)}) collective-permute-start(f32[192,128]{1,0:T(8,128)S(1)} %bitcast.406), channel_id=1, source_target_pairs={{2,0},{4,2},{6,4},{8,6},{10,8},{12,10},{14,12},{16,14},{18,16},{20... | collective-permute-start | bytes 294920 | tf_op jit(solution)/shard_map/ppermute | solution.py:20
  61.1 3.9 %collective-permute-start.9 = (f32[192,128]{1,0:T(8,128)S(1)}, f32[192,128]{1,0:T(8,128)S(1)}, u32[]{:S(2)}, u32[]{:S(2)}) collective-permute-start(f32[192,128]{1,0:T(8,128)S(1)} %bitcast.407), channel_id=1, source_target_pairs={{2,0},{4,2},{6,4},{8,6},{10,8},{12,10},{14,12},{16,14},{18,16},{20... | collective-permute-start | bytes 294920 | tf_op jit(solution)/shard_map/ppermute | solution.py:20
  70.2 2.6 collective-permute-start.10
  72.8 3.9 %collective-permute-start.11 = (f32[192,128]{1,0:T(8,128)S(1)}, f32[192,128]{1,0:T(8,128)S(1)}, u32[]{:S(2)}, u32[]{:S(2)}) collective-permute-start(f32[192,128]{1,0:T(8,128)S(1)} %bitcast.408), channel_id=1, source_target_pairs={{2,0},{4,2},{6,4},{8,6},{10,8},{12,10},{14,12},{16,14},{18,16},{20... | collective-permute-start | bytes 294920 | tf_op jit(solution)/shard_map/ppermute | solution.py:20
  81.9 2.6 collective-permute-start.12
  84.6 3.9 %collective-permute-start.13 = (f32[192,128]{1,0:T(8,128)S(1)}, f32[192,128]{1,0:T(8,128)S(1)}, u32[]{:S(2)}, u32[]{:S(2)}) collective-permute-start(f32[192,128]{1,0:T(8,128)S(1)} %bitcast.409), channel_id=1, source_target_pairs={{2,0},{4,2},{6,4},{8,6},{10,8},{12,10},{14,12},{16,14},{18,16},{20... | collective-permute-start | bytes 294920 | tf_op jit(solution)/shard_map/ppermute | solution.py:20
  93.7 2.6 collective-permute-start.14
  96.3 4.1 %collective-permute-start.15 = (f32[192,128]{1,0:T(8,128)S(1)}, f32[192,128]{1,0:T(8,128)S(1)}, u32[]{:S(2)}, u32[]{:S(2)}) collective-permute-start(f32[192,128]{1,0:T(8,128)S(1)} %bitcast.410), channel_id=1, source_target_pairs={{2,0},{4,2},{6,4},{8,6},{10,8},{12,10},{14,12},{16,14},{18,16},{20... | collective-permute-start | bytes 294920 | tf_op jit(solution)/shard_map/ppermute | solution.py:20
  108.0 3.9 %collective-permute-start.17 = (f32[192,128]{1,0:T(8,128)S(1)}, f32[192,128]{1,0:T(8,128)S(1)}, u32[]{:S(2)}, u32[]{:S(2)}) collective-permute-start(f32[192,128]{1,0:T(8,128)S(1)} %bitcast.402), channel_id=1, source_target_pairs={{2,0},{4,2},{6,4},{8,6},{10,8},{12,10},{14,12},{16,14},{18,16},{20... | collective-permute-start | bytes 294920 | tf_op jit(solution)/shard_map/ppermute | solution.py:20
  117.8 2.6 collective-permute-start.18
  120.4 3.9 %collective-permute-start.19 = (f32[192,128]{1,0:T(8,128)S(1)}, f32[192,128]{1,0:T(8,128)S(1)}, u32[]{:S(2)}, u32[]{:S(2)}) collective-permute-start(f32[192,128]{1,0:T(8,128)S(1)} %bitcast.411), channel_id=1, source_target_pairs={{2,0},{4,2},{6,4},{8,6},{10,8},{12,10},{14,12},{16,14},{18,16},{20... | collective-permute-start | bytes 294920 | tf_op jit(solution)/shard_map/ppermute | solution.py:20
  129.4 2.6 collective-permute-start.20
  132.0 3.9 %collective-permute-start.21 = (f32[192,128]{1,0:T(8,128)S(1)}, f32[192,128]{1,0:T(8,128)S(1)}, u32[]{:S(2)}, u32[]{:S(2)}) collective-permute-start(f32[192,128]{1,0:T(8,128)S(1)} %bitcast.412), channel_id=1, source_target_pairs={{2,0},{4,2},{6,4},{8,6},{10,8},{12,10},{14,12},{16,14},{18,16},{20... | collective-permute-start | bytes 294920 | tf_op jit(solution)/shard_map/ppermute | solution.py:20
  141.1 2.6 collective-permute-start.22
  143.8 3.9 %collective-permute-start.23 = (f32[192,128]{1,0:T(8,128)S(1)}, f32[192,128]{1,0:T(8,128)S(1)}, u32[]{:S(2)}, u32[]{:S(2)}) collective-permute-start(f32[192,128]{1,0:T(8,128)S(1)} %bitcast.413), channel_id=1, source_target_pairs={{2,0},{4,2},{6,4},{8,6},{10,8},{12,10},{14,12},{16,14},{18,16},{20... | collective-permute-start | bytes 294920 | tf_op jit(solution)/shard_map/ppermute | solution.py:20
  152.9 2.6 collective-permute-start.24
  155.5 3.9 %collective-permute-start.25 = (f32[192,128]{1,0:T(8,128)S(1)}, f32[192,128]{1,0:T(8,128)S(1)}, u32[]{:S(2)}, u32[]{:S(2)}) collective-permute-start(f32[192,128]{1,0:T(8,128)S(1)} %bitcast.414), channel_id=1, source_target_pairs={{2,0},{4,2},{6,4},{8,6},{10,8},{12,10},{14,12},{16,14},{18,16},{20... | collective-permute-start | bytes 294920 | tf_op jit(solution)/shard_map/ppermute | solution.py:20
  164.6 2.6 collective-permute-start.26
  167.2 3.9 %collective-permute-start.27 = (f32[192,128]{1,0:T(8,128)S(1)}, f32[192,128]{1,0:T(8,128)S(1)}, u32[]{:S(2)}, u32[]{:S(2)}) collective-permute-start(f32[192,128]{1,0:T(8,128)S(1)} %bitcast.415), channel_id=1, source_target_pairs={{2,0},{4,2},{6,4},{8,6},{10,8},{12,10},{14,12},{16,14},{18,16},{20... | collective-permute-start | bytes 294920 | tf_op jit(solution)/shard_map/ppermute | solution.py:20
  176.4 2.6 collective-permute-start.28
  179.0 3.9 %collective-permute-start.29 = (f32[192,128]{1,0:T(8,128)S(1)}, f32[192,128]{1,0:T(8,128)S(1)}, u32[]{:S(2)}, u32[]{:S(2)}) collective-permute-start(f32[192,128]{1,0:T(8,128)S(1)} %bitcast.416), channel_id=1, source_target_pairs={{2,0},{4,2},{6,4},{8,6},{10,8},{12,10},{14,12},{16,14},{18,16},{20... | collective-permute-start | bytes 294920 | tf_op jit(solution)/shard_map/ppermute | solution.py:20
  188.1 2.6 collective-permute-start.30
  190.7 4.2 %collective-permute-start.31 = (f32[192,128]{1,0:T(8,128)S(1)}, f32[192,128]{1,0:T(8,128)S(1)}, u32[]{:S(2)}, u32[]{:S(2)}) collective-permute-start(f32[192,128]{1,0:T(8,128)S(1)} %bitcast.417), channel_id=1, source_target_pairs={{2,0},{4,2},{6,4},{8,6},{10,8},{12,10},{14,12},{16,14},{18,16},{20... | collective-permute-start | bytes 294920 | tf_op jit(solution)/shard_map/ppermute | solution.py:20
  199.8 2.6 collective-permute-start.32
  202.5 3.9 %collective-permute-start.33 = (f32[192,128]{1,0:T(8,128)S(1)}, f32[192,128]{1,0:T(8,128)S(1)}, u32[]{:S(2)}, u32[]{:S(2)}) collective-permute-start(f32[192,128]{1,0:T(8,128)S(1)} %bitcast.399), channel_id=1, source_target_pairs={{2,0},{4,2},{6,4},{8,6},{10,8},{12,10},{14,12},{16,14},{18,16},{20... | collective-permute-start | bytes 294920 | tf_op jit(solution)/shard_map/ppermute | solution.py:20
  210.5 2.6 collective-permute-start.34
  213.2 3.9 %collective-permute-start.35 = (f32[192,128]{1,0:T(8,128)S(1)}, f32[192,128]{1,0:T(8,128)S(1)}, u32[]{:S(2)}, u32[]{:S(2)}) collective-permute-start(f32[192,128]{1,0:T(8,128)S(1)} %bitcast.400), channel_id=1, source_target_pairs={{2,0},{4,2},{6,4},{8,6},{10,8},{12,10},{14,12},{16,14},{18,16},{20... | collective-permute-start | bytes 294920 | tf_op jit(solution)/shard_map/ppermute | solution.py:20
  225.7 88.6 %all-reduce.3.cloned.1.call-done = f32[64,2,128]{2,0,1:T(8,128)} async-done(((f32[64,2,128]{2,0,1:T(8,128)}), f32[64,2,128]{2,0,1:T(8,128)}) %all-reduce.3.cloned.1.call-update) | async-done | bytes 65552
  315.1 6.3 %all_to_all.5 = f32[2,2,2,128]{3,1,2,0:T(2,128)S(1)} all-to-all(f32[2,2,2,128]{3,1,2,0:T(2,128)S(1)} %pad_maximum_fusion.18), channel_id=1, replica_groups=mesh['blk'=16,'narrow'=2] {'narrow'}, dimensions={0} | all-to-all | bytes 8192 | tf_op jit(solution)/shard_map/all_to_all | solution.py:63
  (169 shorter events, 112.2 us)
Async XLA Ops:
  7.2 307.1 %all-reduce.3.cloned.1.call-start = ((), (), s32[]{:S(2)}) async-start(), calls=%async_computation.1 | async-start | bytes 131072
  8.7 10.9 %collective-permute-start = (f32[192,128]{1,0:T(8,128)S(1)}, f32[192,128]{1,0:T(8,128)S(1)}, u32[]{:S(2)}, u32[]{:S(2)}) collective-permute-start(f32[192,128]{1,0:T(8,128)S(1)} %bitcast.398), channel_id=1, source_target_pairs={{0,2},{2,4},{4,6},{6,8},{8,10},{10,12},{12,14},{14,16},{16,18},{18... | collective-permute-start | bytes 294920 | tf_op jit(solution)/shard_map/ppermute | solution.py:18
  10.6 9.0 %collective-permute-start.1 = (f32[192,128]{1,0:T(8,128)S(1)}, f32[192,128]{1,0:T(8,128)S(1)}, u32[]{:S(2)}, u32[]{:S(2)}) collective-permute-start(f32[192,128]{1,0:T(8,128)S(1)} %bitcast.397), channel_id=1, source_target_pairs={{2,0},{4,2},{6,4},{8,6},{10,8},{12,10},{14,12},{16,14},{18,16},{20... | collective-permute-start | bytes 294920 | tf_op jit(solution)/shard_map/ppermute | solution.py:20
  23.3 6.8 %collective-permute-start.2 = (f32[192,128]{1,0:T(8,128)S(1)}, f32[192,128]{1,0:T(8,128)S(1)}, u32[]{:S(2)}, u32[]{:S(2)}) collective-permute-start(f32[192,128]{1,0:T(8,128)S(1)} %bitcast.419), channel_id=1, source_target_pairs={{0,2},{2,4},{4,6},{6,8},{8,10},{10,12},{12,14},{14,16},{16,18},{18... | collective-permute-start | bytes 294920 | tf_op jit(solution)/shard_map/ppermute | solution.py:18
  25.3 6.7 %collective-permute-start.3 = (f32[192,128]{1,0:T(8,128)S(1)}, f32[192,128]{1,0:T(8,128)S(1)}, u32[]{:S(2)}, u32[]{:S(2)}) collective-permute-start(f32[192,128]{1,0:T(8,128)S(1)} %bitcast.404), channel_id=1, source_target_pairs={{2,0},{4,2},{6,4},{8,6},{10,8},{12,10},{14,12},{16,14},{18,16},{20... | collective-permute-start | bytes 294920 | tf_op jit(solution)/shard_map/ppermute | solution.py:20
  35.0 6.9 %collective-permute-start.4 = (f32[192,128]{1,0:T(8,128)S(1)}, f32[192,128]{1,0:T(8,128)S(1)}, u32[]{:S(2)}, u32[]{:S(2)}) collective-permute-start(f32[192,128]{1,0:T(8,128)S(1)} %bitcast.420), channel_id=1, source_target_pairs={{0,2},{2,4},{4,6},{6,8},{8,10},{10,12},{12,14},{14,16},{16,18},{18... | collective-permute-start | bytes 294920 | tf_op jit(solution)/shard_map/ppermute | solution.py:18
  36.9 6.8 %collective-permute-start.5 = (f32[192,128]{1,0:T(8,128)S(1)}, f32[192,128]{1,0:T(8,128)S(1)}, u32[]{:S(2)}, u32[]{:S(2)}) collective-permute-start(f32[192,128]{1,0:T(8,128)S(1)} %bitcast.405), channel_id=1, source_target_pairs={{2,0},{4,2},{6,4},{8,6},{10,8},{12,10},{14,12},{16,14},{18,16},{20... | collective-permute-start | bytes 294920 | tf_op jit(solution)/shard_map/ppermute | solution.py:20
  46.7 6.9 %collective-permute-start.6 = (f32[192,128]{1,0:T(8,128)S(1)}, f32[192,128]{1,0:T(8,128)S(1)}, u32[]{:S(2)}, u32[]{:S(2)}) collective-permute-start(f32[192,128]{1,0:T(8,128)S(1)} %bitcast.421), channel_id=1, source_target_pairs={{0,2},{2,4},{4,6},{6,8},{8,10},{10,12},{12,14},{14,16},{16,18},{18... | collective-permute-start | bytes 294920 | tf_op jit(solution)/shard_map/ppermute | solution.py:18
  49.4 6.1 %collective-permute-start.7 = (f32[192,128]{1,0:T(8,128)S(1)}, f32[192,128]{1,0:T(8,128)S(1)}, u32[]{:S(2)}, u32[]{:S(2)}) collective-permute-start(f32[192,128]{1,0:T(8,128)S(1)} %bitcast.406), channel_id=1, source_target_pairs={{2,0},{4,2},{6,4},{8,6},{10,8},{12,10},{14,12},{16,14},{18,16},{20... | collective-permute-start | bytes 294920 | tf_op jit(solution)/shard_map/ppermute | solution.py:20
  58.5 6.9 %collective-permute-start.8 = (f32[192,128]{1,0:T(8,128)S(1)}, f32[192,128]{1,0:T(8,128)S(1)}, u32[]{:S(2)}, u32[]{:S(2)}) collective-permute-start(f32[192,128]{1,0:T(8,128)S(1)} %bitcast.422), channel_id=1, source_target_pairs={{0,2},{2,4},{4,6},{6,8},{8,10},{10,12},{12,14},{14,16},{16,18},{18... | collective-permute-start | bytes 294920 | tf_op jit(solution)/shard_map/ppermute | solution.py:18
  61.1 6.1 %collective-permute-start.9 = (f32[192,128]{1,0:T(8,128)S(1)}, f32[192,128]{1,0:T(8,128)S(1)}, u32[]{:S(2)}, u32[]{:S(2)}) collective-permute-start(f32[192,128]{1,0:T(8,128)S(1)} %bitcast.407), channel_id=1, source_target_pairs={{2,0},{4,2},{6,4},{8,6},{10,8},{12,10},{14,12},{16,14},{18,16},{20... | collective-permute-start | bytes 294920 | tf_op jit(solution)/shard_map/ppermute | solution.py:20
  70.2 6.9 %collective-permute-start.10 = (f32[192,128]{1,0:T(8,128)S(1)}, f32[192,128]{1,0:T(8,128)S(1)}, u32[]{:S(2)}, u32[]{:S(2)}) collective-permute-start(f32[192,128]{1,0:T(8,128)S(1)} %bitcast.423), channel_id=1, source_target_pairs={{0,2},{2,4},{4,6},{6,8},{8,10},{10,12},{12,14},{14,16},{16,18},{18... | collective-permute-start | bytes 294920 | tf_op jit(solution)/shard_map/ppermute | solution.py:18
  72.8 6.1 %collective-permute-start.11 = (f32[192,128]{1,0:T(8,128)S(1)}, f32[192,128]{1,0:T(8,128)S(1)}, u32[]{:S(2)}, u32[]{:S(2)}) collective-permute-start(f32[192,128]{1,0:T(8,128)S(1)} %bitcast.408), channel_id=1, source_target_pairs={{2,0},{4,2},{6,4},{8,6},{10,8},{12,10},{14,12},{16,14},{18,16},{20... | collective-permute-start | bytes 294920 | tf_op jit(solution)/shard_map/ppermute | solution.py:20
  81.9 6.9 %collective-permute-start.12 = (f32[192,128]{1,0:T(8,128)S(1)}, f32[192,128]{1,0:T(8,128)S(1)}, u32[]{:S(2)}, u32[]{:S(2)}) collective-permute-start(f32[192,128]{1,0:T(8,128)S(1)} %bitcast.424), channel_id=1, source_target_pairs={{0,2},{2,4},{4,6},{6,8},{8,10},{10,12},{12,14},{14,16},{16,18},{18... | collective-permute-start | bytes 294920 | tf_op jit(solution)/shard_map/ppermute | solution.py:18
  84.6 6.1 %collective-permute-start.13 = (f32[192,128]{1,0:T(8,128)S(1)}, f32[192,128]{1,0:T(8,128)S(1)}, u32[]{:S(2)}, u32[]{:S(2)}) collective-permute-start(f32[192,128]{1,0:T(8,128)S(1)} %bitcast.409), channel_id=1, source_target_pairs={{2,0},{4,2},{6,4},{8,6},{10,8},{12,10},{14,12},{16,14},{18,16},{20... | collective-permute-start | bytes 294920 | tf_op jit(solution)/shard_map/ppermute | solution.py:20
  93.7 6.9 %collective-permute-start.14 = (f32[192,128]{1,0:T(8,128)S(1)}, f32[192,128]{1,0:T(8,128)S(1)}, u32[]{:S(2)}, u32[]{:S(2)}) collective-permute-start(f32[192,128]{1,0:T(8,128)S(1)} %bitcast.425), channel_id=1, source_target_pairs={{0,2},{2,4},{4,6},{6,8},{8,10},{10,12},{12,14},{14,16},{16,18},{18... | collective-permute-start | bytes 294920 | tf_op jit(solution)/shard_map/ppermute | solution.py:18
  96.3 6.1 %collective-permute-start.15 = (f32[192,128]{1,0:T(8,128)S(1)}, f32[192,128]{1,0:T(8,128)S(1)}, u32[]{:S(2)}, u32[]{:S(2)}) collective-permute-start(f32[192,128]{1,0:T(8,128)S(1)} %bitcast.410), channel_id=1, source_target_pairs={{2,0},{4,2},{6,4},{8,6},{10,8},{12,10},{14,12},{16,14},{18,16},{20... | collective-permute-start | bytes 294920 | tf_op jit(solution)/shard_map/ppermute | solution.py:20
  105.4 7.2 %collective-permute-start.16 = (f32[192,128]{1,0:T(8,128)S(1)}, f32[192,128]{1,0:T(8,128)S(1)}, u32[]{:S(2)}, u32[]{:S(2)}) collective-permute-start(f32[192,128]{1,0:T(8,128)S(1)} %bitcast.418), channel_id=1, source_target_pairs={{0,2},{2,4},{4,6},{6,8},{8,10},{10,12},{12,14},{14,16},{16,18},{18... | collective-permute-start | bytes 294920 | tf_op jit(solution)/shard_map/ppermute | solution.py:18
  108.0 6.1 %collective-permute-start.17 = (f32[192,128]{1,0:T(8,128)S(1)}, f32[192,128]{1,0:T(8,128)S(1)}, u32[]{:S(2)}, u32[]{:S(2)}) collective-permute-start(f32[192,128]{1,0:T(8,128)S(1)} %bitcast.402), channel_id=1, source_target_pairs={{2,0},{4,2},{6,4},{8,6},{10,8},{12,10},{14,12},{16,14},{18,16},{20... | collective-permute-start | bytes 294920 | tf_op jit(solution)/shard_map/ppermute | solution.py:20
  117.8 6.9 %collective-permute-start.18 = (f32[192,128]{1,0:T(8,128)S(1)}, f32[192,128]{1,0:T(8,128)S(1)}, u32[]{:S(2)}, u32[]{:S(2)}) collective-permute-start(f32[192,128]{1,0:T(8,128)S(1)} %bitcast.426), channel_id=1, source_target_pairs={{0,2},{2,4},{4,6},{6,8},{8,10},{10,12},{12,14},{14,16},{16,18},{18... | collective-permute-start | bytes 294920 | tf_op jit(solution)/shard_map/ppermute | solution.py:18
  129.4 6.9 %collective-permute-start.20 = (f32[192,128]{1,0:T(8,128)S(1)}, f32[192,128]{1,0:T(8,128)S(1)}, u32[]{:S(2)}, u32[]{:S(2)}) collective-permute-start(f32[192,128]{1,0:T(8,128)S(1)} %bitcast.427), channel_id=1, source_target_pairs={{0,2},{2,4},{4,6},{6,8},{8,10},{10,12},{12,14},{14,16},{16,18},{18... | collective-permute-start | bytes 294920 | tf_op jit(solution)/shard_map/ppermute | solution.py:18
  141.1 6.9 %collective-permute-start.22 = (f32[192,128]{1,0:T(8,128)S(1)}, f32[192,128]{1,0:T(8,128)S(1)}, u32[]{:S(2)}, u32[]{:S(2)}) collective-permute-start(f32[192,128]{1,0:T(8,128)S(1)} %bitcast.428), channel_id=1, source_target_pairs={{0,2},{2,4},{4,6},{6,8},{8,10},{10,12},{12,14},{14,16},{16,18},{18... | collective-permute-start | bytes 294920 | tf_op jit(solution)/shard_map/ppermute | solution.py:18
  152.9 6.9 %collective-permute-start.24 = (f32[192,128]{1,0:T(8,128)S(1)}, f32[192,128]{1,0:T(8,128)S(1)}, u32[]{:S(2)}, u32[]{:S(2)}) collective-permute-start(f32[192,128]{1,0:T(8,128)S(1)} %bitcast.429), channel_id=1, source_target_pairs={{0,2},{2,4},{4,6},{6,8},{8,10},{10,12},{12,14},{14,16},{16,18},{18... | collective-permute-start | bytes 294920 | tf_op jit(solution)/shard_map/ppermute | solution.py:18
  164.6 6.9 %collective-permute-start.26 = (f32[192,128]{1,0:T(8,128)S(1)}, f32[192,128]{1,0:T(8,128)S(1)}, u32[]{:S(2)}, u32[]{:S(2)}) collective-permute-start(f32[192,128]{1,0:T(8,128)S(1)} %bitcast.430), channel_id=1, source_target_pairs={{0,2},{2,4},{4,6},{6,8},{8,10},{10,12},{12,14},{14,16},{16,18},{18... | collective-permute-start | bytes 294920 | tf_op jit(solution)/shard_map/ppermute | solution.py:18
  167.2 6.1 %collective-permute-start.27 = (f32[192,128]{1,0:T(8,128)S(1)}, f32[192,128]{1,0:T(8,128)S(1)}, u32[]{:S(2)}, u32[]{:S(2)}) collective-permute-start(f32[192,128]{1,0:T(8,128)S(1)} %bitcast.415), channel_id=1, source_target_pairs={{2,0},{4,2},{6,4},{8,6},{10,8},{12,10},{14,12},{16,14},{18,16},{20... | collective-permute-start | bytes 294920 | tf_op jit(solution)/shard_map/ppermute | solution.py:20
  176.4 6.9 %collective-permute-start.28 = (f32[192,128]{1,0:T(8,128)S(1)}, f32[192,128]{1,0:T(8,128)S(1)}, u32[]{:S(2)}, u32[]{:S(2)}) collective-permute-start(f32[192,128]{1,0:T(8,128)S(1)} %bitcast.431), channel_id=1, source_target_pairs={{0,2},{2,4},{4,6},{6,8},{8,10},{10,12},{12,14},{14,16},{16,18},{18... | collective-permute-start | bytes 294920 | tf_op jit(solution)/shard_map/ppermute | solution.py:18
  179.0 6.1 %collective-permute-start.29 = (f32[192,128]{1,0:T(8,128)S(1)}, f32[192,128]{1,0:T(8,128)S(1)}, u32[]{:S(2)}, u32[]{:S(2)}) collective-permute-start(f32[192,128]{1,0:T(8,128)S(1)} %bitcast.416), channel_id=1, source_target_pairs={{2,0},{4,2},{6,4},{8,6},{10,8},{12,10},{14,12},{16,14},{18,16},{20... | collective-permute-start | bytes 294920 | tf_op jit(solution)/shard_map/ppermute | solution.py:20
  188.1 6.9 %collective-permute-start.30 = (f32[192,128]{1,0:T(8,128)S(1)}, f32[192,128]{1,0:T(8,128)S(1)}, u32[]{:S(2)}, u32[]{:S(2)}) collective-permute-start(f32[192,128]{1,0:T(8,128)S(1)} %bitcast.432), channel_id=1, source_target_pairs={{0,2},{2,4},{4,6},{6,8},{8,10},{10,12},{12,14},{14,16},{16,18},{18... | collective-permute-start | bytes 294920 | tf_op jit(solution)/shard_map/ppermute | solution.py:18
  190.7 6.1 %collective-permute-start.31 = (f32[192,128]{1,0:T(8,128)S(1)}, f32[192,128]{1,0:T(8,128)S(1)}, u32[]{:S(2)}, u32[]{:S(2)}) collective-permute-start(f32[192,128]{1,0:T(8,128)S(1)} %bitcast.417), channel_id=1, source_target_pairs={{2,0},{4,2},{6,4},{8,6},{10,8},{12,10},{14,12},{16,14},{18,16},{20... | collective-permute-start | bytes 294920 | tf_op jit(solution)/shard_map/ppermute | solution.py:20
  199.8 7.3 %collective-permute-start.32 = (f32[192,128]{1,0:T(8,128)S(1)}, f32[192,128]{1,0:T(8,128)S(1)}, u32[]{:S(2)}, u32[]{:S(2)}) collective-permute-start(f32[192,128]{1,0:T(8,128)S(1)} %bitcast.401), channel_id=1, source_target_pairs={{0,2},{2,4},{4,6},{6,8},{8,10},{10,12},{12,14},{14,16},{16,18},{18... | collective-permute-start | bytes 294920 | tf_op jit(solution)/shard_map/ppermute | solution.py:18
  202.5 6.1 %collective-permute-start.33 = (f32[192,128]{1,0:T(8,128)S(1)}, f32[192,128]{1,0:T(8,128)S(1)}, u32[]{:S(2)}, u32[]{:S(2)}) collective-permute-start(f32[192,128]{1,0:T(8,128)S(1)} %bitcast.399), channel_id=1, source_target_pairs={{2,0},{4,2},{6,4},{8,6},{10,8},{12,10},{14,12},{16,14},{18,16},{20... | collective-permute-start | bytes 294920 | tf_op jit(solution)/shard_map/ppermute | solution.py:20
  210.5 6.9 %collective-permute-start.34 = (f32[192,128]{1,0:T(8,128)S(1)}, f32[192,128]{1,0:T(8,128)S(1)}, u32[]{:S(2)}, u32[]{:S(2)}) collective-permute-start(f32[192,128]{1,0:T(8,128)S(1)} %bitcast.403), channel_id=1, source_target_pairs={{0,2},{2,4},{4,6},{6,8},{8,10},{10,12},{12,14},{14,16},{16,18},{18... | collective-permute-start | bytes 294920 | tf_op jit(solution)/shard_map/ppermute | solution.py:18
  (15 other events, 155.9 us)
Sparse Core Ops, SparseCore 0:
  223.9 90.2 all-reduce.2
